TPU v7x, 512 devices: a whole 4x8x8 slice. The times are simulated.
512 devices in a mesh: pipe: 4 (over z_hi, core), seq: 128 (over y, x, z_lo).
Axes of the slice: x: 4, y: 8, z: 8 (z_hi: 2, z_lo: 4; z = z_hi * 4 + z_lo), core: 2. Of those that a mesh axis runs over, the one named last changes fastest.
Arguments:
- layer_input: bfloat16 [4, 16384, 256], P('pipe', 'seq'), may hold values from -6 to 6
- filters: float32 [4, 16384, 256], P('pipe', 'seq'), may hold values from -1 to 1
- skip: float32 [4, 256], P('pipe'), may hold values from 0.5 to 1.5
- incoming: bfloat16 [4, 16384, 256], P('pipe', 'seq'), may hold values from -6 to 6
- loss_grad: bfloat16 [16384, 256], P('seq'), may hold values from -6 to 6
Outputs:
- input_grad: bfloat16 [4, 16384, 256], P('pipe', 'seq')
- filter_grad: float32 [4, 16384, 256], P('pipe', 'seq')
All inputs are finite; a program needn't handle non-finite values.
Results may differ from a plain program's by a relative error of at most 0.001.
Values may be sent and summed in bfloat16 or wider, within the bound.
No kernel may reach another device: no remote copies, remote signals or barrier semaphores. Data moves between devices by JAX's collectives and lax.ppermute only.
A program may use at most 64 MiB of HBM per device.

v0:
```python
import math

import jax
import jax.numpy as jnp
from jax import lax
from jax.sharding import PartitionSpec as P

HIGHEST = lax.Precision.HIGHEST


def passed_along(block, axis, distance):
    devices = range(lax.axis_size(axis))
    route = [(i - distance, i) for i in devices if i - distance in devices]
    return lax.ppermute(block, axis, route)


def angle_table(left, right, modulus):
    product = left * right % modulus
    angle = product.astype(jnp.float32) * (2.0 * math.pi / modulus)
    return (jnp.cos(angle), jnp.sin(angle))


def forward_spectrum(signals):
    parts = lax.axis_size("seq")
    rows = signals.shape[1]
    block = rows // parts
    total = 2 * parts * rows
    place = lax.axis_index("seq")
    gathered = lax.all_to_all(signals[:, None], "seq", split_axis=2, concat_axis=1, tiled=True)
    freq_ids = lax.broadcasted_iota(jnp.int32, (2 * parts, parts), 0)
    class_ids = lax.broadcasted_iota(jnp.int32, (2 * parts, parts), 1)
    cos_tab, sin_tab = angle_table(freq_ids, class_ids, 2 * parts)
    real = jnp.einsum("rq,kqjc->krjc", cos_tab, gathered, precision=HIGHEST)
    imag = -jnp.einsum("rq,kqjc->krjc", sin_tab, gathered, precision=HIGHEST)
    freq_grid = lax.broadcasted_iota(jnp.int32, (1, 2 * parts, block, 1), 1)
    row_grid = place * block + lax.broadcasted_iota(jnp.int32, (1, 2 * parts, block, 1), 2)
    tw_cos, tw_sin = angle_table(freq_grid, row_grid, total)
    segment_real = real * tw_cos + imag * tw_sin
    segment_imag = imag * tw_cos - real * tw_sin
    real = lax.all_to_all(segment_real, "seq", split_axis=1, concat_axis=2, tiled=True)
    imag = lax.all_to_all(segment_imag, "seq", split_axis=1, concat_axis=2, tiled=True)
    out_ids = lax.broadcasted_iota(jnp.int32, (rows, rows), 0)
    row_ids = lax.broadcasted_iota(jnp.int32, (rows, rows), 1)
    cos_tab, sin_tab = angle_table(out_ids, row_ids, rows)
    out_real = jnp.einsum("sj,kmjc->kmsc", cos_tab, real, precision=HIGHEST) + jnp.einsum(
        "sj,kmjc->kmsc", sin_tab, imag, precision=HIGHEST
    )
    out_imag = jnp.einsum("sj,kmjc->kmsc", cos_tab, imag, precision=HIGHEST) - jnp.einsum(
        "sj,kmjc->kmsc", sin_tab, real, precision=HIGHEST
    )
    return (out_real, out_imag)


def inverse_signal(real, imag):
    parts = lax.axis_size("seq")
    rows = real.shape[2]
    total = 2 * parts * rows
    place = lax.axis_index("seq")
    row_ids = lax.broadcasted_iota(jnp.int32, (rows, rows), 0)
    out_ids = lax.broadcasted_iota(jnp.int32, (rows, rows), 1)
    cos_tab, sin_tab = angle_table(row_ids, out_ids, rows)
    part_real = jnp.einsum("js,kmsc->kmjc", cos_tab, real, precision=HIGHEST) - jnp.einsum(
        "js,kmsc->kmjc", sin_tab, imag, precision=HIGHEST
    )
    part_imag = jnp.einsum("js,kmsc->kmjc", sin_tab, real, precision=HIGHEST) + jnp.einsum(
        "js,kmsc->kmjc", cos_tab, imag, precision=HIGHEST
    )
    freq_grid = 2 * place + lax.broadcasted_iota(jnp.int32, (1, 2, rows, 1), 1)
    row_grid = lax.broadcasted_iota(jnp.int32, (1, 2, rows, 1), 2)
    tw_cos, tw_sin = angle_table(freq_grid, row_grid, total)
    turned_real = part_real * tw_cos - part_imag * tw_sin
    turned_imag = part_real * tw_sin + part_imag * tw_cos
    gath_real = lax.all_to_all(turned_real, "seq", split_axis=2, concat_axis=1, tiled=True)
    gath_imag = lax.all_to_all(turned_imag, "seq", split_axis=2, concat_axis=1, tiled=True)
    class_ids = lax.broadcasted_iota(jnp.int32, (parts, 2 * parts), 0)
    freq_ids = lax.broadcasted_iota(jnp.int32, (parts, 2 * parts), 1)
    cos_q, sin_q = angle_table(class_ids, freq_ids, 2 * parts)
    factor = 1.0 / total
    value_real = (
        jnp.einsum("qr,krjc->kqjc", cos_q, gath_real, precision=HIGHEST)
        - jnp.einsum("qr,krjc->kqjc", sin_q, gath_imag, precision=HIGHEST)
    ) * factor
    return lax.all_to_all(value_real, "seq", split_axis=1, concat_axis=2, tiled=True)


def per_device(layer_input, filters, skip, incoming, loss_grad):
    received = passed_along(incoming, "pipe", -1)
    is_last = lax.axis_index("pipe") == lax.axis_size("pipe") - 1
    grad_out = jnp.where(is_last, loss_grad[None], received)
    rows = layer_input.shape[1]
    seq_total = rows * lax.axis_size("seq")
    inputs = layer_input[0].astype(jnp.float32)
    grad_vals = grad_out[0].astype(jnp.float32)
    spec_real, spec_imag = forward_spectrum(jnp.stack([inputs, filters[0], grad_vals]))
    in_real, filt_real, grad_real = (spec_real[0], spec_real[1], spec_real[2])
    in_imag, filt_imag, grad_imag = (spec_imag[0], spec_imag[1], spec_imag[2])
    scale = 1.0 / math.sqrt(seq_total)
    adj_real = filt_real * grad_real + filt_imag * grad_imag
    adj_imag = filt_real * grad_imag - filt_imag * grad_real
    corr_real = (grad_real * in_real + grad_imag * in_imag) * scale
    corr_imag = (grad_imag * in_real - grad_real * in_imag) * scale
    results = inverse_signal(jnp.stack([adj_real, corr_real]), jnp.stack([adj_imag, corr_imag]))
    conv_grad = results[0, 0]
    filt_grad = results[1, 0]
    input_grad = (conv_grad + skip[0][None, :] * grad_vals).astype(jnp.bfloat16)
    return (input_grad[None], filt_grad[None])


def solution(mesh):
    return jax.shard_map(
        per_device,
        mesh=mesh,
        in_specs=(
            P("pipe", "seq", None),
            P("pipe", "seq", None),
            P("pipe", None),
            P("pipe", "seq", None),
            P("seq", None),
        ),
        out_specs=(P("pipe", "seq", None), P("pipe", "seq", None)),
        check_vma=False,
    )
```

profile of v0, /device:TPU:1, one launch (start us, length us, event | category | flops | bytes accessed | tf_op | source)
XLA Modules:
  0.0 189.4 jit_solution(257859183745010168)
XLA Ops:
  0.6 8.7 %collective-permute-start = (bf16[1,128,256]{2,1,0:T(8,128)(2,1)}, bf16[1,128,256]{2,1,0:T(8,128)(2,1)S(1)}, u32[]{:S(2)}, u32[]{:S(2)}) collective-permute-start(bf16[1,128,256]{2,1,0:T(8,128)(2,1)} %param.8), channel_id=1, source_target_pairs={{128,0},{256,128},{384,256},{129,1},{257,129},{385,257},{130,2},{2... | collective-permute-start | bytes 196616 | tf_op jit(solution)/shard_map/ppermute | solution.py:14
  9.4 0.0 copy-start.1
  9.4 0.9 convert_element_type.63
  10.3 0.0 copy-start
  10.3 4.6 %collective-permute-done = bf16[1,128,256]{2,1,0:T(8,128)(2,1)S(1)} collective-permute-done((bf16[1,128,256]{2,1,0:T(8,128)(2,1)}, bf16[1,128,256]{2,1,0:T(8,128)(2,1)S(1)}, u32[]{:S(2)}, u32[]{:S(2)}) %collective-permute-start) | collective-permute-done | bytes 65568 | tf_op jit(solution)/shard_map/ppermute | solution.py:14
  14.9 1.1 copy.66
  16.1 14.2 %all-to-all-start = ((f32[3,1,128,256]{3,1,0,2:T(1,128)}), f32[3,1,128,256]{3,1,0,2:T(1,128)S(1)}, u32[]{:S(2)}, u32[]{:S(2)}) async-start(f32[3,1,128,256]{3,1,0,2:T(1,128)} %copy.66), calls=%async_computation | async-start | bytes 786432 | tf_op jit(solution)/shard_map/all_to_all | solution.py:29
  30.3 0.1 fusion.77
  30.3 13.6 %all-to-all-done = f32[3,1,128,256]{3,1,0,2:T(1,128)S(1)} async-done(((f32[3,1,128,256]{3,1,0,2:T(1,128)}), f32[3,1,128,256]{3,1,0,2:T(1,128)S(1)}, u32[]{:S(2)}, u32[]{:S(2)}) %all-to-all-start) | async-done | bytes 393248 | tf_op jit(solution)/shard_map/all_to_all | solution.py:29
  43.9 0.6 copy.67
  44.5 1.3 fusion.2
  45.8 1.3 add_bitcast_fusion
  47.1 1.8 copy.68
  48.9 6.2 %all-to-all-start.1 = ((f32[3,256,1,256]{3,2,0,1:T(1,128)}), f32[3,256,1,256]{3,2,0,1:T(1,128)S(1)}, u32[]{:S(2)}, u32[]{:S(2)}) async-start(f32[3,256,1,256]{3,2,0,1:T(1,128)} %copy.68), calls=%async_computation.1 | async-start | bytes 1572864 | tf_op jit(solution)/shard_map/all_to_all | solution.py:40
  55.1 1.8 copy.71
  56.9 19.2 %all-to-all-done.1 = f32[3,256,1,256]{3,2,0,1:T(1,128)S(1)} async-done(((f32[3,256,1,256]{3,2,0,1:T(1,128)}), f32[3,256,1,256]{3,2,0,1:T(1,128)S(1)}, u32[]{:S(2)}, u32[]{:S(2)}) %all-to-all-start.1) | async-done | bytes 786464 | tf_op jit(solution)/shard_map/all_to_all | solution.py:40
  76.1 6.4 %all-to-all-start.2 = ((f32[3,256,1,256]{3,2,0,1:T(1,128)}), f32[3,256,1,256]{3,2,0,1:T(1,128)S(1)}, u32[]{:S(2)}, u32[]{:S(2)}) async-start(f32[3,256,1,256]{3,2,0,1:T(1,128)} %copy.71), calls=%async_computation.2 | async-start | bytes 1572864 | tf_op jit(solution)/shard_map/all_to_all | solution.py:41
  82.5 0.1 fusion.76
  82.6 0.5 copy.69
  83.1 0.5 copy.70
  83.6 1.0 fusion.6
  84.6 22.6 %all-to-all-done.2 = f32[3,256,1,256]{3,2,0,1:T(1,128)S(1)} async-done(((f32[3,256,1,256]{3,2,0,1:T(1,128)}), f32[3,256,1,256]{3,2,0,1:T(1,128)S(1)}, u32[]{:S(2)}, u32[]{:S(2)}) %all-to-all-start.2) | async-done | bytes 786464 | tf_op jit(solution)/shard_map/all_to_all | solution.py:41
  107.2 0.5 copy.72
  107.8 0.5 copy.73
  108.3 1.0 fusion.8
  109.3 1.0 fusion.1
  110.3 1.0 fusion
  111.4 0.1 multiply_subtract_fusion
  111.5 0.8 fusion.15
  112.3 0.8 fusion.14
  113.2 0.8 convolution_add_fusion.1
  114.0 0.9 add_bitcast_fusion.1
  114.9 1.0 copy.74
  115.9 6.7 %all-to-all-start.3 = ((f32[2,2,128,256]{3,1,0,2:T(2,128)}), f32[2,2,128,256]{3,1,0,2:T(2,128)S(1)}, u32[]{:S(2)}, u32[]{:S(2)}) async-start(f32[2,2,128,256]{3,1,0,2:T(2,128)} %copy.74), calls=%async_computation.3 | async-start | bytes 1048576 | tf_op jit(solution)/shard_map/all_to_all | solution.py:73
  122.6 1.0 copy.77
  123.6 17.1 %all-to-all-done.3 = f32[2,2,128,256]{3,1,0,2:T(2,128)S(1)} async-done(((f32[2,2,128,256]{3,1,0,2:T(2,128)}), f32[2,2,128,256]{3,1,0,2:T(2,128)S(1)}, u32[]{:S(2)}, u32[]{:S(2)}) %all-to-all-start.3) | async-done | bytes 524320 | tf_op jit(solution)/shard_map/all_to_all | solution.py:73
  140.7 7.4 %all-to-all-start.4 = ((f32[2,2,128,256]{3,1,0,2:T(2,128)}), f32[2,2,128,256]{3,1,0,2:T(2,128)S(1)}, u32[]{:S(2)}, u32[]{:S(2)}) async-start(f32[2,2,128,256]{3,1,0,2:T(2,128)} %copy.77), calls=%async_computation.4 | async-start | bytes 1048576 | tf_op jit(solution)/shard_map/all_to_all | solution.py:74
  148.1 0.3 copy.75
  148.4 1.3 fusion.12
  149.7 15.3 %all-to-all-done.4 = f32[2,2,128,256]{3,1,0,2:T(2,128)S(1)} async-done(((f32[2,2,128,256]{3,1,0,2:T(2,128)}), f32[2,2,128,256]{3,1,0,2:T(2,128)S(1)}, u32[]{:S(2)}, u32[]{:S(2)}) %all-to-all-start.4) | async-done | bytes 524320 | tf_op jit(solution)/shard_map/all_to_all | solution.py:74
  165.0 0.3 copy.78
  165.3 1.3 fusion.4
  166.7 0.2 copy.80
  166.9 20.3 %all_to_all.84 = f32[2,128,1,256]{3,2,0,1:T(1,128)S(1)} all-to-all(f32[2,128,1,256]{3,2,0,1:T(1,128)S(1)} %copy.80), channel_id=1, replica_groups=mesh['pipe'=4,'seq'=128] {'seq'}, dimensions={1} | all-to-all | bytes 524288 | tf_op jit(solution)/shard_map/all_to_all | solution.py:83
  187.2 0.2 slice_bitcast_fusion
  187.4 0.7 copy.82
  188.0 0.7 copy-done.2
  188.7 0.7 fusion.25
  (6 shorter events, 0.1 us)
Async XLA Ops:
  0.6 14.2 %collective-permute-start = (bf16[1,128,256]{2,1,0:T(8,128)(2,1)}, bf16[1,128,256]{2,1,0:T(8,128)(2,1)S(1)}, u32[]{:S(2)}, u32[]{:S(2)}) collective-permute-start(bf16[1,128,256]{2,1,0:T(8,128)(2,1)} %param.8), channel_id=1, source_target_pairs={{128,0},{256,128},{384,256},{129,1},{257,129},{385,257},{130,2},{2... | collective-permute-start | bytes 196616 | tf_op jit(solution)/shard_map/ppermute | solution.py:14
  9.4 5.5 %copy-start.1 = (bf16[128,256]{1,0:T(8,128)(2,1)S(1)}, bf16[128,256]{1,0:T(8,128)(2,1)}, u32[]{:S(2)}) copy-start(bf16[128,256]{1,0:T(8,128)(2,1)} %param.9) | copy-start | bytes 196612
  10.3 4.6 %copy-start = (f32[1,128,256]{2,1,0:T(8,128)S(1)}, f32[1,128,256]{2,1,0:T(8,128)}, u32[]{:S(2)}) copy-start(f32[1,128,256]{2,1,0:T(8,128)} %param.6) | copy-start | bytes 393220
  16.1 27.8 %all-to-all-start = ((f32[3,1,128,256]{3,1,0,2:T(1,128)}), f32[3,1,128,256]{3,1,0,2:T(1,128)S(1)}, u32[]{:S(2)}, u32[]{:S(2)}) async-start(f32[3,1,128,256]{3,1,0,2:T(1,128)} %copy.66), calls=%async_computation | async-start | bytes 786432 | tf_op jit(solution)/shard_map/all_to_all | solution.py:29
  48.9 27.2 %all-to-all-start.1 = ((f32[3,256,1,256]{3,2,0,1:T(1,128)}), f32[3,256,1,256]{3,2,0,1:T(1,128)S(1)}, u32[]{:S(2)}, u32[]{:S(2)}) async-start(f32[3,256,1,256]{3,2,0,1:T(1,128)} %copy.68), calls=%async_computation.1 | async-start | bytes 1572864 | tf_op jit(solution)/shard_map/all_to_all | solution.py:40
  76.1 31.2 %all-to-all-start.2 = ((f32[3,256,1,256]{3,2,0,1:T(1,128)}), f32[3,256,1,256]{3,2,0,1:T(1,128)S(1)}, u32[]{:S(2)}, u32[]{:S(2)}) async-start(f32[3,256,1,256]{3,2,0,1:T(1,128)} %copy.71), calls=%async_computation.2 | async-start | bytes 1572864 | tf_op jit(solution)/shard_map/all_to_all | solution.py:41
  115.9 24.8 %all-to-all-start.3 = ((f32[2,2,128,256]{3,1,0,2:T(2,128)}), f32[2,2,128,256]{3,1,0,2:T(2,128)S(1)}, u32[]{:S(2)}, u32[]{:S(2)}) async-start(f32[2,2,128,256]{3,1,0,2:T(2,128)} %copy.74), calls=%async_computation.3 | async-start | bytes 1048576 | tf_op jit(solution)/shard_map/all_to_all | solution.py:73
  140.7 24.4 %all-to-all-start.4 = ((f32[2,2,128,256]{3,1,0,2:T(2,128)}), f32[2,2,128,256]{3,1,0,2:T(2,128)S(1)}, u32[]{:S(2)}, u32[]{:S(2)}) async-start(f32[2,2,128,256]{3,1,0,2:T(2,128)} %copy.77), calls=%async_computation.4 | async-start | bytes 1048576 | tf_op jit(solution)/shard_map/all_to_all | solution.py:74
  188.0 0.7 copy-start.2
where the time goes:
time: 192 us; the launch traced here: 189 us
  waiting for transfers between devices  92.4 us (48%)
  starting transfers between devices  49.5 us (26%)
  blocking collectives  20.3 us (11%)
  matrix products  12.7 us (7%)
  local copies, waits for them, and re-layouts  11.6 us (6%)
    all_to_all x1, waiting for transfers between devices, forward_spectrum(): lax.all_to_all(segment_imag, 'seq', split_axis=1, concat_axis=2, tiled=True)  22.6 us
    all_to_all x1, blocking collectives, inverse_signal(): lax.all_to_all(value_real, 'seq', split_axis=1, concat_axis=2, tiled=True)  20.3 us
    all_to_all x1, waiting for transfers between devices, forward_spectrum(): lax.all_to_all(segment_real, 'seq', split_axis=1, concat_axis=2, tiled=True)  19.2 us
    all_to_all x1, waiting for transfers between devices, inverse_signal(): lax.all_to_all(turned_real, 'seq', split_axis=2, concat_axis=1, tiled=True)  17.1 us
    all_to_all x1, waiting for transfers between devices, inverse_signal(): lax.all_to_all(turned_imag, 'seq', split_axis=2, concat_axis=1, tiled=True)  15.3 us
    all_to_all x1, starting transfers between devices, forward_spectrum(): lax.all_to_all(signals[:, None], 'seq', split_axis=2, concat_axis=1, tile...  14.2 us
    all_to_all x1, waiting for transfers between devices, forward_spectrum(): lax.all_to_all(signals[:, None], 'seq', split_axis=2, concat_axis=1, tile...  13.6 us
    ppermute x1, starting transfers between devices, passed_along(): return lax.ppermute(block, axis, route)  8.75 us
  transfers between devices with their start and end apart: 6, of which 6 were waited for; matrix products, arithmetic and copies ran while one was open for 4% of the time, Pallas kernels for 0%

commit v1 on v0

v1 whole, which is shorter than its diff:
```python
import math

import jax
import jax.numpy as jnp
import numpy as np
from jax import lax
from jax.experimental import pallas as pl
from jax.experimental.pallas import tpu as pltpu
from jax.sharding import PartitionSpec as P

BF16 = jnp.bfloat16
F32 = jnp.float32
BLOCK = 128
LENGTH = BLOCK * BLOCK
ROWS = 8
VMEM = pl.BlockSpec(memory_space=pltpu.VMEM)
SMEM = pl.BlockSpec(memory_space=pltpu.SMEM)


def halves(table):
    high = table.astype(BF16)
    low = (table - high.astype(np.float64)).astype(BF16)
    return (high, low)


def tables():
    q = np.arange(BLOCK)
    first = 2.0 * math.pi * np.outer(q + 0.25, q) / BLOCK
    twist = 2.0 * math.pi * np.outer(q + 0.25, q) / LENGTH
    second = 2.0 * math.pi * (np.outer(q, q) % BLOCK) / BLOCK
    gather = np.concatenate([np.cos(first), -np.sin(first)], axis=0)
    turn_re = np.tile(np.cos(twist), (1, 2)).astype(np.float32)
    turn_im = np.tile(-np.sin(twist), (1, 2)).astype(np.float32)
    cos, sin = (np.cos(second), -np.sin(second))
    mix = np.block([[cos, sin], [-sin, cos]])
    spread = gather.T / LENGTH
    return (halves(gather), (turn_re, turn_im), halves(mix), halves(mix.T), halves(spread))


def split(value):
    high = value.astype(BF16)
    return (high, (value - high.astype(F32)).astype(BF16))


def dot(left, right):
    return jnp.dot(left, right, preferred_element_type=F32)


def dot3(left, right):
    return dot(left[0], right[0]) + dot(left[0], right[1]) + dot(left[1], right[0])


def pack_kernel(where_ref, x_ref, f_ref, skip_ref, inc_ref, loss_ref, out_ref, rows_ref):
    at_start = jnp.where(where_ref[0] == 0, 1.0, 0.0)
    row = lax.broadcasted_iota(jnp.int32, (BLOCK, BLOCK), 0)
    first_row = jnp.where(row == 0, at_start, 0.0)
    use_loss = where_ref[1] == 0
    for half in range(2):
        lanes = slice(half * BLOCK, (half + 1) * BLOCK)
        rows_ref[pl.ds(half, BLOCK, stride=ROWS), :] = x_ref[:, lanes].astype(F32).T
        taps = f_ref[:, lanes] + first_row * skip_ref[:, lanes]
        high = taps.astype(BF16).astype(F32)
        rows_ref[pl.ds(2 + half, BLOCK, stride=ROWS), :] = high.T
        rows_ref[pl.ds(4 + half, BLOCK, stride=ROWS), :] = (taps - high).T
        grad = jnp.where(use_loss, loss_ref[:, lanes].astype(F32), inc_ref[:, lanes].astype(F32))
        rows_ref[pl.ds(6 + half, BLOCK, stride=ROWS), :] = grad.T
    out_ref[...] = rows_ref[...].astype(BF16)


def part_kernel(in_ref, own_ref, grad_ref, rows_ref):
    rows_ref[...] = in_ref[...].astype(F32)
    for r in range(6):
        own_ref[:, r * BLOCK : (r + 1) * BLOCK] = rows_ref[pl.ds(r, BLOCK, stride=ROWS), :].astype(BF16)
    for r in range(2):
        grad_ref[:, r * BLOCK : (r + 1) * BLOCK] = rows_ref[pl.ds(6 + r, BLOCK, stride=ROWS), :].astype(BF16)


def to_spectrum(high, low, gather, turn, mix):
    part = dot(gather[0], high) + dot(gather[1], high)
    if low is not None:
        part = part + dot(gather[0], low)
    real, imag = (part[:BLOCK], part[BLOCK:])
    turned_re = real * turn[0] - imag * turn[1]
    turned_im = real * turn[1] + imag * turn[0]
    stacked = jnp.concatenate(
        [
            jnp.concatenate([turned_re[:, :BLOCK], turned_im[:, :BLOCK]], axis=1),
            jnp.concatenate([turned_re[:, BLOCK:], turned_im[:, BLOCK:]], axis=1),
        ],
        axis=0,
    )
    return dot3(split(stacked), mix)


def forward_kernel(own_ref, gh_ref, gl_ref, tr_ref, ti_ref, mh_ref, ml_ref, u_ref, h_ref):
    gather = (gh_ref[...], gl_ref[...])
    turn = (tr_ref[...], ti_ref[...])
    mix = (mh_ref[...], ml_ref[...])
    width = 2 * BLOCK
    u_ref[...] = to_spectrum(own_ref[:, :width], None, gather, turn, mix)
    h_ref[...] = to_spectrum(own_ref[:, width : 2 * width], own_ref[:, 2 * width :], gather, turn, mix)


def back_kernel(
    grad_ref, u_ref, h_ref, gh_ref, gl_ref, tr_ref, ti_ref, mh_ref, ml_ref, bh_ref, bl_ref, sh_ref, sl_ref, out_ref, rows_ref
):
    turn = (tr_ref[...], ti_ref[...])
    grad = to_spectrum(grad_ref[...], None, (gh_ref[...], gl_ref[...]), turn, (mh_ref[...], ml_ref[...]))
    g_re, g_im = (grad[:, :BLOCK], grad[:, BLOCK:])
    back = (bh_ref[...], bl_ref[...])
    spread = (sh_ref[...], sl_ref[...])
    for index, other in enumerate((h_ref, u_ref)):
        o_re, o_im = (other[:, :BLOCK], other[:, BLOCK:])
        product = jnp.concatenate([o_re * g_re + o_im * g_im, o_re * g_im - o_im * g_re], axis=1)
        part = dot3(split(product), back)
        real = jnp.concatenate([part[:BLOCK, :BLOCK], part[BLOCK:, :BLOCK]], axis=1)
        imag = jnp.concatenate([part[:BLOCK, BLOCK:], part[BLOCK:, BLOCK:]], axis=1)
        stacked = jnp.concatenate([real * turn[0] + imag * turn[1], imag * turn[0] - real * turn[1]], axis=0)
        value = dot3(spread, split(stacked))
        for half in range(2):
            one = value[:, half * BLOCK : (half + 1) * BLOCK]
            if index == 0:
                rows_ref[pl.ds(half, BLOCK, stride=ROWS), :] = one
            else:
                one = one * (1.0 / math.sqrt(LENGTH))
                high = one.astype(BF16).astype(F32)
                rows_ref[pl.ds(2 + half, BLOCK, stride=ROWS), :] = high
                rows_ref[pl.ds(4 + half, BLOCK, stride=ROWS), :] = one - high
                rows_ref[pl.ds(6 + half, BLOCK, stride=ROWS), :] = jnp.zeros_like(one)
    out_ref[...] = rows_ref[...].astype(BF16)


def unpack_kernel(in_ref, grad_ref, filt_ref, rows_ref):
    rows_ref[...] = in_ref[...].astype(F32)
    for half in range(2):
        lanes = slice(half * BLOCK, (half + 1) * BLOCK)
        grad_ref[:, lanes] = rows_ref[pl.ds(half, BLOCK, stride=ROWS), :].T.astype(BF16)
        both = rows_ref[pl.ds(2 + half, BLOCK, stride=ROWS), :] + rows_ref[pl.ds(4 + half, BLOCK, stride=ROWS), :]
        filt_ref[:, lanes] = both.T


def shape(rows, columns, kind):
    return jax.ShapeDtypeStruct((rows, columns), kind)


def call(kernel, outs, ins, scratch=()):
    return pl.pallas_call(
        kernel,
        out_shape=outs,
        in_specs=ins,
        out_specs=jax.tree.map(lambda _: VMEM, outs),
        scratch_shapes=scratch,
    )


ROW_SCRATCH = (pltpu.VMEM((ROWS * BLOCK, BLOCK), F32),)
WIDE = 2 * BLOCK


def exchanged(packed):
    blocks = packed.reshape(BLOCK, ROWS, BLOCK)
    blocks = lax.all_to_all(blocks, "seq", split_axis=0, concat_axis=0, tiled=True)
    return blocks.reshape(ROWS * BLOCK, BLOCK)


def per_device(layer_input, filters, skip, incoming, loss_grad):
    gather, turn, mix, back, spread = tables()
    where = jnp.stack([lax.axis_index("seq"), lax.axis_index("pipe")]).astype(jnp.int32)
    packed = call(pack_kernel, shape(ROWS * BLOCK, BLOCK, BF16), [SMEM] + [VMEM] * 5, ROW_SCRATCH)(
        where, layer_input[0], filters[0], skip, incoming[0], loss_grad
    )
    received = exchanged(packed)
    own, grad = call(part_kernel, (shape(BLOCK, 3 * WIDE, BF16), shape(BLOCK, WIDE, BF16)), [VMEM], ROW_SCRATCH)(received)
    parts = lax.axis_size("pipe")
    grad = lax.ppermute(grad, "pipe", [(i, (i - 1) % parts) for i in range(parts)])
    spectrum = shape(WIDE, WIDE, F32)
    forward = (*gather, *turn, *mix)
    u_spec, h_spec = call(forward_kernel, (spectrum, spectrum), [VMEM] * 7)(own, *forward)
    results = call(back_kernel, shape(ROWS * BLOCK, BLOCK, BF16), [VMEM] * 13, ROW_SCRATCH)(
        grad, u_spec, h_spec, *forward, *back, *spread
    )
    arrived = exchanged(results)
    input_grad, filter_grad = call(unpack_kernel, (shape(BLOCK, WIDE, BF16), shape(BLOCK, WIDE, F32)), [VMEM], ROW_SCRATCH)(arrived)
    return (input_grad[None], filter_grad[None])


def solution(mesh):
    return jax.shard_map(
        per_device,
        mesh=mesh,
        in_specs=(
            P("pipe", "seq", None),
            P("pipe", "seq", None),
            P("pipe", None),
            P("pipe", "seq", None),
            P("seq", None),
        ),
        out_specs=(P("pipe", "seq", None), P("pipe", "seq", None)),
        check_vma=False,
    )
```

time: 192 us -> 76.1 us (0.40); the launches traced: 189 us -> 75.8 us
  waiting for transfers between devices: 92.4 us -> 6.07 us
  starting transfers between devices: 49.5 us -> 4.94 us
  blocking collectives: 20.3 us -> 51.2 us
  matrix products: 12.7 us -> 0 us
  Pallas kernels: 0 us -> 11.7 us
  local copies, waits for them, and re-layouts: 11.6 us -> 0.63 us
    all_to_all x5 -> x0, waiting for transfers between devices: 87.9 us -> none  [the longest x1 22.6 us: forward_spectrum(): lax.all_to_all(segment_imag, 'seq', split_axis=1, concat_axis=2, tiled=True)]
    all_to_all x5 -> x0, starting transfers between devices: 40.8 us -> none  [the longest x1 14.2 us: forward_spectrum(): lax.all_to_all(signals[:, None], 'seq', split_axis=2, concat_axis=1, tile...]
    all_to_all x1 -> x2, blocking collectives: 20.3 us -> 51.2 us  [exchanged(): lax.all_to_all(blocks, 'seq', split_axis=0, concat_axis=0, tiled=True)]
    dot_general x12 -> x0, matrix products: 12.7 us -> none  [the longest x1 1.34 us: inverse_signal(): jnp.einsum('qr,krjc->kqjc', sin_q, gath_imag, precision=HIGHEST)]
    pallas_call x0 -> x5, Pallas kernels: none -> 11.7 us  [the longest x1 3.61 us: per_device(): call(back_kernel, shape(ROWS * BLOCK, BLOCK, BF16), [VMEM] * 13, ROW_SCRA...]
    ppermute x1, starting transfers between devices: 8.75 us -> 4.94 us  [per_device(): lax.ppermute(grad, 'pipe', [(i, (i - 1) % parts) for i in range(parts)])]
    all_to_all x7 -> x0, local copies, waits for them, and re-layouts: 3.16 us -> none  [the longest x2 1.03 us: forward_spectrum(): lax.all_to_all(segment_real, 'seq', split_axis=1, concat_axis=2, tiled=True)]
    add x2 -> x0, local copies, waits for them, and re-layouts: 2.79 us -> none  [the longest x1 1.79 us: forward_spectrum(): segment_real = real * tw_cos + imag * tw_sin]
  transfers between devices with their start and end apart: 6 -> 1, of which waited for: 6 -> 1; matrix products, arithmetic and copies ran while one was open for 4% -> 0% of each run, Pallas kernels for 0% -> 4%
where the time goes in v1:
time: 76.1 us; the launch traced here: 75.8 us
  blocking collectives  51.2 us (67%)
  Pallas kernels  11.7 us (15%)
  waiting for transfers between devices  6.07 us (8%)
  starting transfers between devices  4.94 us (6%)
    all_to_all x2, blocking collectives, exchanged(): lax.all_to_all(blocks, 'seq', split_axis=0, concat_axis=0, tiled=True)  51.2 us
    ppermute x1, waiting for transfers between devices, per_device(): lax.ppermute(grad, 'pipe', [(i, (i - 1) % parts) for i in range(parts)])  6.07 us
    ppermute x1, starting transfers between devices, per_device(): lax.ppermute(grad, 'pipe', [(i, (i - 1) % parts) for i in range(parts)])  4.94 us
    pallas_call x1, Pallas kernels, per_device(): call(back_kernel, shape(ROWS * BLOCK, BLOCK, BF16), [VMEM] * 13, ROW_SCRA...  3.61 us
    pallas_call x1, Pallas kernels, per_device(): call(forward_kernel, (spectrum, spectrum), [VMEM] * 7)(own, *forward)  2.69 us
    pallas_call x1, Pallas kernels, per_device(): call(pack_kernel, shape(ROWS * BLOCK, BLOCK, BF16), [SMEM] + [VMEM] * 5,...  1.88 us
    pallas_call x1, Pallas kernels, per_device(): call(part_kernel, (shape(BLOCK, 3 * WIDE, BF16), shape(BLOCK, WIDE, BF16)...  1.77 us
    pallas_call x1, Pallas kernels, per_device(): call(unpack_kernel, (shape(BLOCK, WIDE, BF16), shape(BLOCK, WIDE, F32)),...  1.76 us
  transfers between devices with their start and end apart: 1, of which 1 were waited for; matrix products, arithmetic and copies ran while one was open for 0% of the time, Pallas kernels for 4%

profile of v1, /device:TPU:1, one launch (start us, length us, event | category | flops | bytes accessed | tf_op | source)
XLA Modules:
  0.0 75.8 jit_solution(916766747968512547)
XLA Ops:
  0.6 0.6 pad_add_fusion.where_ref
  1.2 1.9 %shard_map.158 = bf16[1024,128]{1,0:T(8,128)(2,1)} custom-call(s32[2]{0:T(128)} %pad_add_fusion.where_ref, bf16[128,256]{1,0:T(8,128)(2,1)} %bitcast.16, f32[128,256]{1,0:T(8,128)} %bitcast.15, f32[1,256]{1,0:T(1,128)} %skip_ref.1, bf16[128,256]{1,0:T(8,128)(2,1)} %bitcast.17, bf16[128,256]{1,0:T(8,128)(2,1)} %loss_ref.1), custom_call_target="tpu_custom_call" | custom-call | tf_op jit(solution)/shard_map/pallas_call | solution.py:169
  3.1 30.9 %all_to_all.10 = bf16[128,8,128]{2,1,0:T(8,128)(2,1)} all-to-all(bf16[128,8,128]{2,1,0:T(8,128)(2,1)} %bitcast.13), channel_id=1, replica_groups=mesh['pipe'=4,'seq'=128] {'seq'}, dimensions={0} | all-to-all | bytes 524288 | tf_op jit(solution)/shard_map/all_to_all | solution.py:162
  34.0 1.8 %shard_map.159 = (bf16[128,768]{1,0:T(8,128)(2,1)}, bf16[128,256]{1,0:T(8,128)(2,1)}) custom-call(bf16[1024,128]{1,0:T(8,128)(2,1)} %bitcast.11), custom_call_target="tpu_custom_call" | custom-call | tf_op jit(solution)/shard_map/pallas_call | solution.py:173
  35.8 4.9 %collective-permute-start = (bf16[128,256]{1,0:T(8,128)(2,1)}, bf16[128,256]{1,0:T(8,128)(2,1)S(1)}, u32[]{:S(2)}, u32[]{:S(2)}) collective-permute-start(bf16[128,256]{1,0:T(8,128)(2,1)} %get-tuple-element.8), channel_id=1, source_target_pairs={{0,384},{128,0},{256,128},{384,256},{1,385},{129,1},{257,129},{385... | collective-permute-start | bytes 196616 | tf_op jit(solution)/shard_map/ppermute | solution.py:175
  40.7 2.7 %shard_map.160 = (f32[256,256]{1,0:T(8,128)}, f32[256,256]{1,0:T(8,128)}) custom-call(bf16[128,768]{1,0:T(8,128)(2,1)} %get-tuple-element.9.own_ref, bf16[256,128]{1,0:T(8,128)(2,1)} %constant.29.clone.gh_ref, bf16[256,128]{1,0:T(8,128)(2,1)} %constant.30.clone.gl_ref, f32[128,256]{1,0:T(8,128)} %constant.31.clone.tr_ref, f32[128,256]{1,0:T(8,128)} %constant.32.clone.ti_ref, ...), custom_call_target="tpu_custom_call" | custom-call | tf_op jit(solution)/shard_map/pallas_call | solution.py:178
  43.4 6.1 %collective-permute-done.grad_ref = bf16[128,256]{1,0:T(8,128)(2,1)S(1)} collective-permute-done((bf16[128,256]{1,0:T(8,128)(2,1)}, bf16[128,256]{1,0:T(8,128)(2,1)S(1)}, u32[]{:S(2)}, u32[]{:S(2)}) %collective-permute-start) | collective-permute-done | bytes 65568 | tf_op jit(solution)/shard_map/ppermute | solution.py:175
  49.5 0.0 copy-start
  49.5 0.6 copy-done
  50.1 3.6 %shard_map.161 = bf16[1024,128]{1,0:T(8,128)(2,1)} custom-call(bf16[128,256]{1,0:T(8,128)(2,1)} %copy-done, f32[256,256]{1,0:T(8,128)} %get-tuple-element.10.u_ref, f32[256,256]{1,0:T(8,128)} %get-tuple-element.11.h_ref, bf16[256,128]{1,0:T(8,128)(2,1)} %constant.29.clone.gh_ref, bf16[256,128]{1,0:T(8,128)(2,1)} %constant.30.clone.gl_ref, ...), custom_call_target="tpu_custom_call" | custom-call | tf_op jit(solution)/shard_map/pallas_call | solution.py:179
  53.8 20.2 %all_to_all.11 = bf16[128,8,128]{2,1,0:T(8,128)(2,1)} all-to-all(bf16[128,8,128]{2,1,0:T(8,128)(2,1)} %bitcast.14), channel_id=1, replica_groups=mesh['pipe'=4,'seq'=128] {'seq'}, dimensions={0} | all-to-all | bytes 524288 | tf_op jit(solution)/shard_map/all_to_all | solution.py:162
  74.0 1.8 %shard_map.162 = (bf16[128,256]{1,0:T(8,128)(2,1)}, f32[128,256]{1,0:T(8,128)}) custom-call(bf16[1024,128]{1,0:T(8,128)(2,1)} %bitcast.12), custom_call_target="tpu_custom_call" | custom-call | tf_op jit(solution)/shard_map/pallas_call | solution.py:183
Async XLA Ops:
  35.8 13.7 %collective-permute-start = (bf16[128,256]{1,0:T(8,128)(2,1)}, bf16[128,256]{1,0:T(8,128)(2,1)S(1)}, u32[]{:S(2)}, u32[]{:S(2)}) collective-permute-start(bf16[128,256]{1,0:T(8,128)(2,1)} %get-tuple-element.8), channel_id=1, source_target_pairs={{0,384},{128,0},{256,128},{384,256},{1,385},{129,1},{257,129},{385... | collective-permute-start | bytes 196616 | tf_op jit(solution)/shard_map/ppermute | solution.py:175
  49.5 0.6 copy-start

commit v2 on v1

--- a/solution.py
+++ b/solution.py
@@ -50,29 +50,27 @@
     return dot(left[0], right[0]) + dot(left[0], right[1]) + dot(left[1], right[0])
 
 
-def pack_kernel(where_ref, x_ref, f_ref, skip_ref, inc_ref, loss_ref, out_ref, rows_ref):
-    at_start = jnp.where(where_ref[0] == 0, 1.0, 0.0)
+def pack_kernel(x_ref, f_ref, skip_ref, rows_ref):
+    at_start = jnp.where(lax.axis_index("seq") == 0, 1.0, 0.0)
     row = lax.broadcasted_iota(jnp.int32, (BLOCK, BLOCK), 0)
     first_row = jnp.where(row == 0, at_start, 0.0)
-    use_loss = where_ref[1] == 0
     for half in range(2):
         lanes = slice(half * BLOCK, (half + 1) * BLOCK)
         rows_ref[pl.ds(half, BLOCK, stride=ROWS), :] = x_ref[:, lanes].astype(F32).T
-        taps = f_ref[:, lanes] + first_row * skip_ref[:, lanes]
+        taps = (f_ref[:, lanes] + first_row * skip_ref[:, lanes]).T
         high = taps.astype(BF16).astype(F32)
-        rows_ref[pl.ds(2 + half, BLOCK, stride=ROWS), :] = high.T
-        rows_ref[pl.ds(4 + half, BLOCK, stride=ROWS), :] = (taps - high).T
-        grad = jnp.where(use_loss, loss_ref[:, lanes].astype(F32), inc_ref[:, lanes].astype(F32))
-        rows_ref[pl.ds(6 + half, BLOCK, stride=ROWS), :] = grad.T
-    out_ref[...] = rows_ref[...].astype(BF16)
+        rows_ref[pl.ds(2 + half, BLOCK, stride=ROWS), :] = high
+        rows_ref[pl.ds(4 + half, BLOCK, stride=ROWS), :] = taps - high
 
 
-def part_kernel(in_ref, own_ref, grad_ref, rows_ref):
-    rows_ref[...] = in_ref[...].astype(F32)
-    for r in range(6):
-        own_ref[:, r * BLOCK : (r + 1) * BLOCK] = rows_ref[pl.ds(r, BLOCK, stride=ROWS), :].astype(BF16)
-    for r in range(2):
-        grad_ref[:, r * BLOCK : (r + 1) * BLOCK] = rows_ref[pl.ds(6 + r, BLOCK, stride=ROWS), :].astype(BF16)
+def join_kernel(rows_ref, inc_ref, loss_ref, out_ref, all_ref):
+    is_last = lax.axis_index("pipe") == lax.axis_size("pipe") - 1
+    all_ref[...] = rows_ref[...]
+    for half in range(2):
+        lanes = slice(half * BLOCK, (half + 1) * BLOCK)
+        grad = jnp.where(is_last, loss_ref[:, lanes].astype(F32), inc_ref[:, lanes].astype(F32))
+        all_ref[pl.ds(6 + half, BLOCK, stride=ROWS), :] = grad.T
+    out_ref[...] = all_ref[...].astype(BF16)
 
 
 def to_spectrum(high, low, gather, turn, mix):
@@ -92,24 +90,23 @@
     return dot3(split(stacked), mix)
 
 
-def forward_kernel(own_ref, gh_ref, gl_ref, tr_ref, ti_ref, mh_ref, ml_ref, u_ref, h_ref):
+def main_kernel(in_ref, gh_ref, gl_ref, tr_ref, ti_ref, mh_ref, ml_ref, bh_ref, bl_ref, sh_ref, sl_ref, out_ref, rows_ref):
     gather = (gh_ref[...], gl_ref[...])
     turn = (tr_ref[...], ti_ref[...])
     mix = (mh_ref[...], ml_ref[...])
-    width = 2 * BLOCK
-    u_ref[...] = to_spectrum(own_ref[:, :width], None, gather, turn, mix)
-    h_ref[...] = to_spectrum(own_ref[:, width : 2 * width], own_ref[:, 2 * width :], gather, turn, mix)
-
-
-def back_kernel(
-    grad_ref, u_ref, h_ref, gh_ref, gl_ref, tr_ref, ti_ref, mh_ref, ml_ref, bh_ref, bl_ref, sh_ref, sl_ref, out_ref, rows_ref
-):
-    turn = (tr_ref[...], ti_ref[...])
-    grad = to_spectrum(grad_ref[...], None, (gh_ref[...], gl_ref[...]), turn, (mh_ref[...], ml_ref[...]))
-    g_re, g_im = (grad[:, :BLOCK], grad[:, BLOCK:])
     back = (bh_ref[...], bl_ref[...])
     spread = (sh_ref[...], sl_ref[...])
-    for index, other in enumerate((h_ref, u_ref)):
+    rows_ref[...] = in_ref[...].astype(F32)
+
+    def pair(r):
+        both = [rows_ref[pl.ds(r + half, BLOCK, stride=ROWS), :].astype(BF16) for half in range(2)]
+        return jnp.concatenate(both, axis=1)
+
+    grad = to_spectrum(pair(6), None, gather, turn, mix)
+    g_re, g_im = (grad[:, :BLOCK], grad[:, BLOCK:])
+    taps = to_spectrum(pair(2), pair(4), gather, turn, mix)
+    inputs = to_spectrum(pair(0), None, gather, turn, mix)
+    for index, other in enumerate((taps, inputs)):
         o_re, o_im = (other[:, :BLOCK], other[:, BLOCK:])
         product = jnp.concatenate([o_re * g_re + o_im * g_im, o_re * g_im - o_im * g_re], axis=1)
         part = dot3(split(product), back)
@@ -143,44 +140,40 @@
     return jax.ShapeDtypeStruct((rows, columns), kind)
 
 
+def near(value):
+    return pltpu.with_memory_space_constraint(value, pltpu.VMEM)
+
+
 def call(kernel, outs, ins, scratch=()):
     return pl.pallas_call(
         kernel,
         out_shape=outs,
-        in_specs=ins,
+        in_specs=[VMEM] * ins,
         out_specs=jax.tree.map(lambda _: VMEM, outs),
         scratch_shapes=scratch,
     )
 
 
 ROW_SCRATCH = (pltpu.VMEM((ROWS * BLOCK, BLOCK), F32),)
+PACKED = pltpu.VMEM((ROWS * BLOCK, BLOCK), BF16)
 WIDE = 2 * BLOCK
 
 
 def exchanged(packed):
     blocks = packed.reshape(BLOCK, ROWS, BLOCK)
     blocks = lax.all_to_all(blocks, "seq", split_axis=0, concat_axis=0, tiled=True)
-    return blocks.reshape(ROWS * BLOCK, BLOCK)
+    return near(blocks.reshape(ROWS * BLOCK, BLOCK))
 
 
 def per_device(layer_input, filters, skip, incoming, loss_grad):
-    gather, turn, mix, back, spread = tables()
-    where = jnp.stack([lax.axis_index("seq"), lax.axis_index("pipe")]).astype(jnp.int32)
-    packed = call(pack_kernel, shape(ROWS * BLOCK, BLOCK, BF16), [SMEM] + [VMEM] * 5, ROW_SCRATCH)(
-        where, layer_input[0], filters[0], skip, incoming[0], loss_grad
-    )
-    received = exchanged(packed)
-    own, grad = call(part_kernel, (shape(BLOCK, 3 * WIDE, BF16), shape(BLOCK, WIDE, BF16)), [VMEM], ROW_SCRATCH)(received)
+    constants = [near(jnp.asarray(half)) for pair in tables() for half in pair]
     parts = lax.axis_size("pipe")
-    grad = lax.ppermute(grad, "pipe", [(i, (i - 1) % parts) for i in range(parts)])
-    spectrum = shape(WIDE, WIDE, F32)
-    forward = (*gather, *turn, *mix)
-    u_spec, h_spec = call(forward_kernel, (spectrum, spectrum), [VMEM] * 7)(own, *forward)
-    results = call(back_kernel, shape(ROWS * BLOCK, BLOCK, BF16), [VMEM] * 13, ROW_SCRATCH)(
-        grad, u_spec, h_spec, *forward, *back, *spread
-    )
-    arrived = exchanged(results)
-    input_grad, filter_grad = call(unpack_kernel, (shape(BLOCK, WIDE, BF16), shape(BLOCK, WIDE, F32)), [VMEM], ROW_SCRATCH)(arrived)
+    passed = lax.ppermute(incoming[0], "pipe", [(i, i - 1) for i in range(1, parts)])
+    rows = call(pack_kernel, pltpu.VMEM((ROWS * BLOCK, BLOCK), F32), 3)(layer_input[0], filters[0], skip)
+    packed = call(join_kernel, PACKED, 3, ROW_SCRATCH)(near(rows), near(passed), near(loss_grad))
+    results = call(main_kernel, PACKED, 11, ROW_SCRATCH)(exchanged(packed), *constants)
+    outs = (shape(BLOCK, WIDE, BF16), shape(BLOCK, WIDE, F32))
+    input_grad, filter_grad = call(unpack_kernel, outs, 1, ROW_SCRATCH)(exchanged(results))
     return (input_grad[None], filter_grad[None])
 
 

time: 76.1 us -> 62.8 us (0.83)
  Pallas kernels: 11.7 us -> 3.64 us
  blocking collectives: 51.2 us -> 44.9 us
  starting transfers between devices: 4.94 us -> 8.75 us
  waiting for transfers between devices: 6.07 us -> 4.4 us
    pallas_call x5 -> x4, Pallas kernels: 11.7 us -> 3.64 us  [the longest x1 1.61 us: per_device(): call(main_kernel, PACKED, 11, ROW_SCRATCH)(exchanged(packed), *constants)]
    all_to_all x2, blocking collectives: 51.2 us -> 44.9 us  [exchanged(): lax.all_to_all(blocks, 'seq', split_axis=0, concat_axis=0, tiled=True)]
    ppermute x1, starting transfers between devices: 4.94 us -> 8.75 us  [per_device(): lax.ppermute(incoming[0], 'pipe', [(i, i - 1) for i in range(1, parts)])]
    ppermute x1, waiting for transfers between devices: 6.07 us -> 4.4 us  [per_device(): lax.ppermute(incoming[0], 'pipe', [(i, i - 1) for i in range(1, parts)])]
  transfers between devices with their start and end apart: 1 -> 1, of which waited for: 1 -> 1; matrix products, arithmetic and copies ran while one was open for 0% -> 0% of each run, Pallas kernels for 4% -> 2%
where the time goes in v2:
time: 62.8 us; the launch traced here: 62.6 us
  blocking collectives  44.9 us (71%)
  starting transfers between devices  8.75 us (14%)
  waiting for transfers between devices  4.4 us (7%)
  Pallas kernels  3.64 us (6%)
  between operations  0.79 us (1%)
    all_to_all x2, blocking collectives, exchanged(): lax.all_to_all(blocks, 'seq', split_axis=0, concat_axis=0, tiled=True)  44.9 us
    ppermute x1, starting transfers between devices, per_device(): lax.ppermute(incoming[0], 'pipe', [(i, i - 1) for i in range(1, parts)])  8.75 us
    ppermute x1, waiting for transfers between devices, per_device(): lax.ppermute(incoming[0], 'pipe', [(i, i - 1) for i in range(1, parts)])  4.4 us
    pallas_call x1, Pallas kernels, per_device(): call(main_kernel, PACKED, 11, ROW_SCRATCH)(exchanged(packed), *constants)  1.61 us
  transfers between devices with their start and end apart: 1, of which 1 were waited for; matrix products, arithmetic and copies ran while one was open for 0% of the time, Pallas kernels for 2%

profile of v2, /device:TPU:1, one launch (start us, length us, event | category | flops | bytes accessed | tf_op | source)
XLA Modules:
  0.0 62.6 jit_solution(12106298222766940575)
XLA Ops:
  0.6 8.7 %collective-permute-start = (bf16[128,256]{1,0:T(8,128)(2,1)}, bf16[128,256]{1,0:T(8,128)(2,1)S(1)}, u32[]{:S(2)}, u32[]{:S(2)}) collective-permute-start(bf16[128,256]{1,0:T(8,128)(2,1)} %bitcast.16), channel_id=1, source_target_pairs={{128,0},{256,128},{384,256},{129,1},{257,129},{385,257},{130,2},{2... | collective-permute-start | bytes 196616 | tf_op jit(solution)/shard_map/ppermute | solution.py:171
  9.4 0.0 copy-start.6
  9.4 1.1 %shard_map.158.rows_ref = f32[1024,128]{1,0:T(8,128)S(1)} custom-call(bf16[128,256]{1,0:T(8,128)(2,1)} %bitcast.14, f32[128,256]{1,0:T(8,128)} %bitcast.13, f32[1,256]{1,0:T(1,128)} %skip_ref.1), custom_call_target="tpu_custom_call" | custom-call | tf_op jit(solution)/shard_map/pallas_call | solution.py:172
  10.5 4.4 %collective-permute-done.inc_ref = bf16[128,256]{1,0:T(8,128)(2,1)S(1)} collective-permute-done((bf16[128,256]{1,0:T(8,128)(2,1)}, bf16[128,256]{1,0:T(8,128)(2,1)S(1)}, u32[]{:S(2)}, u32[]{:S(2)}) %collective-permute-start) | collective-permute-done | bytes 65568 | tf_op jit(solution)/shard_map/ppermute | solution.py:171
  14.9 0.0 copy-done.6
  14.9 0.0 copy-start.4
  14.9 0.0 copy-start.5
  14.9 0.0 copy-start.7
  14.9 0.0 copy-start.8
  14.9 0.0 copy-start.9
  14.9 0.0 copy-start.10
  14.9 0.1 shard_map.159
  15.1 0.0 copy-start
  15.1 0.0 copy-start.1
  15.1 0.0 copy-start.2
  15.1 0.0 copy-start.3
  15.1 26.7 %all_to_all.10 = bf16[128,8,128]{2,1,0:T(8,128)(2,1)S(1)} all-to-all(bf16[128,8,128]{2,1,0:T(8,128)(2,1)S(1)} %bitcast.9), channel_id=1, replica_groups=mesh['pipe'=4,'seq'=128] {'seq'}, dimensions={0} | all-to-all | bytes 524288 | tf_op jit(solution)/shard_map/all_to_all | solution.py:164
  41.8 0.0 copy-done.4
  41.8 0.0 copy-done.5
  41.8 0.0 copy-done.7
  41.8 0.0 copy-done.8
  41.9 0.0 copy-done.9
  41.9 0.0 copy-done.10
  41.9 0.0 copy-done
  41.9 0.0 copy-done.1
  41.9 0.0 copy-done.2
  41.9 0.0 copy-done.3
  41.9 1.6 %shard_map.160 = bf16[1024,128]{1,0:T(8,128)(2,1)S(1)} custom-call(bf16[1024,128]{1,0:T(8,128)(2,1)S(1)} %bitcast.11, bf16[256,128]{1,0:T(8,128)(2,1)S(1)} %copy-done.10, bf16[256,128]{1,0:T(8,128)(2,1)S(1)} %copy-done.9, f32[128,256]{1,0:T(8,128)S(1)} %copy-done.5, f32[128,256]{1,0:T(8,128)S(1)} %copy-done.4, bf16[256,256]{1,0:T(8,128)(2,1)S(1)} %copy-done.3, ...), custom_call_target="tpu_custom_call" | custom-call | tf_op jit(solution)/shard_map/pallas_call | solution.py:174
  43.5 18.2 %all_to_all.11 = bf16[128,8,128]{2,1,0:T(8,128)(2,1)S(1)} all-to-all(bf16[128,8,128]{2,1,0:T(8,128)(2,1)S(1)} %bitcast.12), channel_id=1, replica_groups=mesh['pipe'=4,'seq'=128] {'seq'}, dimensions={0} | all-to-all | bytes 524288 | tf_op jit(solution)/shard_map/all_to_all | solution.py:164
  61.7 0.8 %shard_map.161 = (bf16[128,256]{1,0:T(8,128)(2,1)}, f32[128,256]{1,0:T(8,128)}) custom-call(bf16[1024,128]{1,0:T(8,128)(2,1)S(1)} %bitcast.10), custom_call_target="tpu_custom_call" | custom-call | tf_op jit(solution)/shard_map/pallas_call | solution.py:176
Async XLA Ops:
  0.6 14.2 %collective-permute-start = (bf16[128,256]{1,0:T(8,128)(2,1)}, bf16[128,256]{1,0:T(8,128)(2,1)S(1)}, u32[]{:S(2)}, u32[]{:S(2)}) collective-permute-start(bf16[128,256]{1,0:T(8,128)(2,1)} %bitcast.16), channel_id=1, source_target_pairs={{128,0},{256,128},{384,256},{129,1},{257,129},{385,257},{130,2},{2... | collective-permute-start | bytes 196616 | tf_op jit(solution)/shard_map/ppermute | solution.py:171
  9.4 5.5 %copy-start.6 = (bf16[128,256]{1,0:T(8,128)(2,1)S(1)}, bf16[128,256]{1,0:T(8,128)(2,1)}, u32[]{:S(2)}) copy-start(bf16[128,256]{1,0:T(8,128)(2,1)} %loss_ref.1) | copy-start | bytes 196612
  14.9 27.0 %copy-start.4 = (f32[128,256]{1,0:T(8,128)S(1)}, f32[128,256]{1,0:T(8,128)}, u32[]{:S(2)}) copy-start(f32[128,256]{1,0:T(8,128)} %constant.23.clone.ti_ref) | copy-start | bytes 393220
  14.9 27.0 %copy-start.5 = (f32[128,256]{1,0:T(8,128)S(1)}, f32[128,256]{1,0:T(8,128)}, u32[]{:S(2)}) copy-start(f32[128,256]{1,0:T(8,128)} %constant.22.clone.tr_ref) | copy-start | bytes 393220
  14.9 27.0 %copy-start.7 = (bf16[128,256]{1,0:T(8,128)(2,1)S(1)}, bf16[128,256]{1,0:T(8,128)(2,1)}, u32[]{:S(2)}) copy-start(bf16[128,256]{1,0:T(8,128)(2,1)} %constant.29.clone.sl_ref) | copy-start | bytes 196612
  14.9 27.0 %copy-start.8 = (bf16[128,256]{1,0:T(8,128)(2,1)S(1)}, bf16[128,256]{1,0:T(8,128)(2,1)}, u32[]{:S(2)}) copy-start(bf16[128,256]{1,0:T(8,128)(2,1)} %constant.28.clone.sh_ref) | copy-start | bytes 196612
  14.9 27.0 %copy-start.9 = (bf16[256,128]{1,0:T(8,128)(2,1)S(1)}, bf16[256,128]{1,0:T(8,128)(2,1)}, u32[]{:S(2)}) copy-start(bf16[256,128]{1,0:T(8,128)(2,1)} %constant.21.clone.gl_ref) | copy-start | bytes 196612
  14.9 27.0 %copy-start.10 = (bf16[256,128]{1,0:T(8,128)(2,1)S(1)}, bf16[256,128]{1,0:T(8,128)(2,1)}, u32[]{:S(2)}) copy-start(bf16[256,128]{1,0:T(8,128)(2,1)} %constant.20.clone.gh_ref) | copy-start | bytes 196612
  15.1 26.8 %copy-start = (bf16[256,256]{1,0:T(8,128)(2,1)S(1)}, bf16[256,256]{1,0:T(8,128)(2,1)}, u32[]{:S(2)}) copy-start(bf16[256,256]{1,0:T(8,128)(2,1)} %constant.27.clone.bl_ref) | copy-start | bytes 393220
  15.1 26.8 %copy-start.1 = (bf16[256,256]{1,0:T(8,128)(2,1)S(1)}, bf16[256,256]{1,0:T(8,128)(2,1)}, u32[]{:S(2)}) copy-start(bf16[256,256]{1,0:T(8,128)(2,1)} %constant.26.clone.bh_ref) | copy-start | bytes 393220
  15.1 26.8 %copy-start.2 = (bf16[256,256]{1,0:T(8,128)(2,1)S(1)}, bf16[256,256]{1,0:T(8,128)(2,1)}, u32[]{:S(2)}) copy-start(bf16[256,256]{1,0:T(8,128)(2,1)} %constant.25.clone.ml_ref) | copy-start | bytes 393220
  15.1 26.8 %copy-start.3 = (bf16[256,256]{1,0:T(8,128)(2,1)S(1)}, bf16[256,256]{1,0:T(8,128)(2,1)}, u32[]{:S(2)}) copy-start(bf16[256,256]{1,0:T(8,128)(2,1)} %constant.24.clone.mh_ref) | copy-start | bytes 393220

commit v3 on v2

--- a/solution.py
+++ b/solution.py
@@ -13,6 +13,8 @@
 BLOCK = 128
 LENGTH = BLOCK * BLOCK
 ROWS = 8
+BACK_ROWS = 6
+ORDER = [int(f"{i:07b}"[::-1], 2) for i in range(BLOCK)]
 VMEM = pl.BlockSpec(memory_space=pltpu.VMEM)
 SMEM = pl.BlockSpec(memory_space=pltpu.SMEM)
 
@@ -25,16 +27,19 @@
 
 def tables():
     q = np.arange(BLOCK)
-    first = 2.0 * math.pi * np.outer(q + 0.25, q) / BLOCK
+    order = np.array(ORDER)
+    first = 2.0 * math.pi * np.outer(q + 0.25, order) / BLOCK
+    moved = 2.0 * math.pi * np.outer(q + 0.25, order ^ 2) / BLOCK
     twist = 2.0 * math.pi * np.outer(q + 0.25, q) / LENGTH
     second = 2.0 * math.pi * (np.outer(q, q) % BLOCK) / BLOCK
     gather = np.concatenate([np.cos(first), -np.sin(first)], axis=0)
+    moved = np.concatenate([np.cos(moved), -np.sin(moved)], axis=0)
     turn_re = np.tile(np.cos(twist), (1, 2)).astype(np.float32)
     turn_im = np.tile(-np.sin(twist), (1, 2)).astype(np.float32)
     cos, sin = (np.cos(second), -np.sin(second))
     mix = np.block([[cos, sin], [-sin, cos]])
     spread = gather.T / LENGTH
-    return (halves(gather), (turn_re, turn_im), halves(mix), halves(mix.T), halves(spread))
+    return (halves(gather), halves(moved), (turn_re, turn_im), halves(mix), halves(mix.T), halves(spread))
 
 
 def split(value):
@@ -90,8 +95,12 @@
     return dot3(split(stacked), mix)
 
 
-def main_kernel(in_ref, gh_ref, gl_ref, tr_ref, ti_ref, mh_ref, ml_ref, bh_ref, bl_ref, sh_ref, sl_ref, out_ref, rows_ref):
+def main_kernel(
+    in_ref, gh_ref, gl_ref, ah_ref, al_ref, tr_ref, ti_ref, mh_ref, ml_ref, bh_ref, bl_ref, sh_ref, sl_ref, out_ref, rows_ref, back_ref
+):
     gather = (gh_ref[...], gl_ref[...])
+    is_moved = lax.axis_index("pipe") == 1
+    moved = (jnp.where(is_moved, ah_ref[...], gather[0]), jnp.where(is_moved, al_ref[...], gather[1]))
     turn = (tr_ref[...], ti_ref[...])
     mix = (mh_ref[...], ml_ref[...])
     back = (bh_ref[...], bl_ref[...])
@@ -102,7 +111,7 @@
         both = [rows_ref[pl.ds(r + half, BLOCK, stride=ROWS), :].astype(BF16) for half in range(2)]
         return jnp.concatenate(both, axis=1)
 
-    grad = to_spectrum(pair(6), None, gather, turn, mix)
+    grad = to_spectrum(pair(6), None, moved, turn, mix)
     g_re, g_im = (grad[:, :BLOCK], grad[:, BLOCK:])
     taps = to_spectrum(pair(2), pair(4), gather, turn, mix)
     inputs = to_spectrum(pair(0), None, gather, turn, mix)
@@ -117,22 +126,21 @@
         for half in range(2):
             one = value[:, half * BLOCK : (half + 1) * BLOCK]
             if index == 0:
-                rows_ref[pl.ds(half, BLOCK, stride=ROWS), :] = one
+                back_ref[pl.ds(half, BLOCK, stride=BACK_ROWS), :] = one
             else:
                 one = one * (1.0 / math.sqrt(LENGTH))
                 high = one.astype(BF16).astype(F32)
-                rows_ref[pl.ds(2 + half, BLOCK, stride=ROWS), :] = high
-                rows_ref[pl.ds(4 + half, BLOCK, stride=ROWS), :] = one - high
-                rows_ref[pl.ds(6 + half, BLOCK, stride=ROWS), :] = jnp.zeros_like(one)
-    out_ref[...] = rows_ref[...].astype(BF16)
+                back_ref[pl.ds(2 + half, BLOCK, stride=BACK_ROWS), :] = high
+                back_ref[pl.ds(4 + half, BLOCK, stride=BACK_ROWS), :] = one - high
+    out_ref[...] = back_ref[...].astype(BF16)
 
 
 def unpack_kernel(in_ref, grad_ref, filt_ref, rows_ref):
     rows_ref[...] = in_ref[...].astype(F32)
     for half in range(2):
         lanes = slice(half * BLOCK, (half + 1) * BLOCK)
-        grad_ref[:, lanes] = rows_ref[pl.ds(half, BLOCK, stride=ROWS), :].T.astype(BF16)
-        both = rows_ref[pl.ds(2 + half, BLOCK, stride=ROWS), :] + rows_ref[pl.ds(4 + half, BLOCK, stride=ROWS), :]
+        grad_ref[:, lanes] = rows_ref[pl.ds(half, BLOCK, stride=BACK_ROWS), :].T.astype(BF16)
+        both = rows_ref[pl.ds(2 + half, BLOCK, stride=BACK_ROWS), :] + rows_ref[pl.ds(4 + half, BLOCK, stride=BACK_ROWS), :]
         filt_ref[:, lanes] = both.T
 
 
@@ -155,25 +163,36 @@
 
 
 ROW_SCRATCH = (pltpu.VMEM((ROWS * BLOCK, BLOCK), F32),)
-PACKED = pltpu.VMEM((ROWS * BLOCK, BLOCK), BF16)
+BACK_SCRATCH = (pltpu.VMEM((BACK_ROWS * BLOCK, BLOCK), F32),)
 WIDE = 2 * BLOCK
 
 
+def packed_rows(rows):
+    return pltpu.VMEM((rows * BLOCK, BLOCK), BF16)
+
+
 def exchanged(packed):
-    blocks = packed.reshape(BLOCK, ROWS, BLOCK)
-    blocks = lax.all_to_all(blocks, "seq", split_axis=0, concat_axis=0, tiled=True)
-    return near(blocks.reshape(ROWS * BLOCK, BLOCK))
+    rows = packed.shape[0] // BLOCK
+    block = (rows, BLOCK) if rows % 8 == 0 else (rows // 2, 2, BLOCK)
+    blocks = packed.reshape(BLOCK, *block)
+    blocks = lax.all_to_all(blocks, "seq", split_axis=0, concat_axis=0, tiled=True, axis_index_groups=[ORDER])
+    return near(blocks.reshape(packed.shape))
+
+
+def route():
+    parts = lax.axis_size("pipe")
+    devices = lax.axis_size("seq")
+    return [(p * devices + q, (p - 1) * devices + (q ^ 2 if p == 2 else q)) for p in range(1, parts) for q in range(devices)]
 
 
 def per_device(layer_input, filters, skip, incoming, loss_grad):
     constants = [near(jnp.asarray(half)) for pair in tables() for half in pair]
-    parts = lax.axis_size("pipe")
-    passed = lax.ppermute(incoming[0], "pipe", [(i, i - 1) for i in range(1, parts)])
+    passed = lax.ppermute(incoming[0], ("pipe", "seq"), route())
     rows = call(pack_kernel, pltpu.VMEM((ROWS * BLOCK, BLOCK), F32), 3)(layer_input[0], filters[0], skip)
-    packed = call(join_kernel, PACKED, 3, ROW_SCRATCH)(near(rows), near(passed), near(loss_grad))
-    results = call(main_kernel, PACKED, 11, ROW_SCRATCH)(exchanged(packed), *constants)
+    packed = call(join_kernel, packed_rows(ROWS), 3, ROW_SCRATCH)(near(rows), near(passed), near(loss_grad))
+    results = call(main_kernel, packed_rows(BACK_ROWS), 13, ROW_SCRATCH + BACK_SCRATCH)(exchanged(packed), *constants)
     outs = (shape(BLOCK, WIDE, BF16), shape(BLOCK, WIDE, F32))
-    input_grad, filter_grad = call(unpack_kernel, outs, 1, ROW_SCRATCH)(exchanged(results))
+    input_grad, filter_grad = call(unpack_kernel, outs, 1, BACK_SCRATCH)(exchanged(results))
     return (input_grad[None], filter_grad[None])
 
 

time: 62.8 us -> 59.9 us (0.954)
  blocking collectives: 44.9 us -> 42 us
    all_to_all x2, blocking collectives: 44.9 us -> 42 us  [exchanged(): lax.all_to_all(blocks, 'seq', split_axis=0, concat_axis=0, tiled=True, ax...]
where the time goes in v3:
time: 59.9 us; the launch traced here: 59.7 us
  blocking collectives  42 us (70%)
  starting transfers between devices  8.75 us (15%)
  waiting for transfers between devices  4.42 us (7%)
  Pallas kernels  3.6 us (6%)
  between operations  0.82 us (1%)
    all_to_all x2, blocking collectives, exchanged(): lax.all_to_all(blocks, 'seq', split_axis=0, concat_axis=0, tiled=True, ax...  42 us
    ppermute x1, starting transfers between devices, per_device(): passed = lax.ppermute(incoming[0], ('pipe', 'seq'), route())  8.75 us
    ppermute x1, waiting for transfers between devices, per_device(): passed = lax.ppermute(incoming[0], ('pipe', 'seq'), route())  4.42 us
    pallas_call x1, Pallas kernels, per_device(): call(main_kernel, packed_rows(BACK_ROWS), 13, ROW_SCRATCH + BACK_SCRATCH)  1.58 us
  transfers between devices with their start and end apart: 1, of which 1 were waited for; matrix products, arithmetic and copies ran while one was open for 0% of the time, Pallas kernels for 2%

profile of v3, /device:TPU:1, one launch (start us, length us, event | category | flops | bytes accessed | tf_op | source)
XLA Modules:
  0.0 59.7 jit_solution(6199488244967975297)
XLA Ops:
  0.6 8.7 %collective-permute-start = (bf16[128,256]{1,0:T(8,128)(2,1)}, bf16[128,256]{1,0:T(8,128)(2,1)S(1)}, u32[]{:S(2)}, u32[]{:S(2)}) collective-permute-start(bf16[128,256]{1,0:T(8,128)(2,1)} %bitcast.16), channel_id=1, source_target_pairs={{128,0},{129,1},{130,2},{131,3},{132,4},{133,5},{134,6},{135,7},{1... | collective-permute-start | bytes 196616 | tf_op jit(solution)/shard_map/ppermute | solution.py:190
  9.4 0.0 copy-start.6
  9.4 1.1 %shard_map.176.rows_ref = f32[1024,128]{1,0:T(8,128)S(1)} custom-call(bf16[128,256]{1,0:T(8,128)(2,1)} %bitcast.14, f32[128,256]{1,0:T(8,128)} %bitcast.13, f32[1,256]{1,0:T(1,128)} %skip_ref.1), custom_call_target="tpu_custom_call" | custom-call | tf_op jit(solution)/shard_map/pallas_call | solution.py:191
  10.5 4.4 %collective-permute-done.inc_ref = bf16[128,256]{1,0:T(8,128)(2,1)S(1)} collective-permute-done((bf16[128,256]{1,0:T(8,128)(2,1)}, bf16[128,256]{1,0:T(8,128)(2,1)S(1)}, u32[]{:S(2)}, u32[]{:S(2)}) %collective-permute-start) | collective-permute-done | bytes 65568 | tf_op jit(solution)/shard_map/ppermute | solution.py:190
  14.9 0.0 copy-done.6
  14.9 0.0 copy-start.4
  14.9 0.0 copy-start.5
  14.9 0.0 copy-start.7
  14.9 0.0 copy-start.8
  14.9 0.0 copy-start.9
  14.9 0.0 copy-start.10
  14.9 0.0 copy-start.11
  15.0 0.0 copy-start.12
  15.0 0.1 shard_map.177
  15.1 0.0 copy-start
  15.1 0.0 copy-start.1
  15.1 0.0 copy-start.2
  15.1 0.0 copy-start.3
  15.2 24.7 %all_to_all.10 = bf16[128,8,128]{2,1,0:T(8,128)(2,1)S(1)} all-to-all(bf16[128,8,128]{2,1,0:T(8,128)(2,1)S(1)} %bitcast.10), channel_id=1, replica_groups={{0,64,32,96,16,80,48,112,8,72,40,104,24,88,56,120,4,68,36,100,20,84,52,..., dimensions={0} | all-to-all | bytes 524288 | tf_op jit(solution)/shard_map/all_to_all | solution.py:178
  39.8 0.0 copy-done.4
  39.8 0.0 copy-done.5
  39.8 0.0 copy-done.7
  39.8 0.0 copy-done.8
  39.9 0.0 copy-done.9
  39.9 0.0 copy-done.10
  39.9 0.0 copy-done.11
  39.9 0.0 copy-done.12
  39.9 0.0 copy-done
  39.9 0.0 copy-done.1
  39.9 0.0 copy-done.2
  39.9 0.0 copy-done.3
  39.9 1.6 %shard_map.178 = bf16[768,128]{1,0:T(8,128)(2,1)S(1)} custom-call(bf16[1024,128]{1,0:T(8,128)(2,1)S(1)} %bitcast.9, bf16[256,128]{1,0:T(8,128)(2,1)S(1)} %copy-done.12, bf16[256,128]{1,0:T(8,128)(2,1)S(1)} %copy-done.11, bf16[256,128]{1,0:T(8,128)(2,1)S(1)} %copy-done.10, bf16[256,128]{1,0:T(8,128)(2,1)S(1)} %copy-done.9, f32[128,256]{1,0:T(8,128)S(1)} %copy-done.5, ...), custom_call_target="tpu_custom_call" | custom-call | tf_op jit(solution)/shard_map/pallas_call | solution.py:193
  41.5 17.4 %all_to_all.11 = bf16[128,3,2,128]{3,2,1,0:T(2,128)(2,1)S(1)} all-to-all(bf16[128,3,2,128]{3,2,1,0:T(2,128)(2,1)S(1)} %bitcast.11), channel_id=1, replica_groups={{0,64,32,96,16,80,48,112,8,72,40,104,24,88,56,120,4,68,36,100,20,84,52,..., dimensions={0} | all-to-all | bytes 393216 | tf_op jit(solution)/shard_map/all_to_all | solution.py:178
  58.9 0.8 %shard_map.179 = (bf16[128,256]{1,0:T(8,128)(2,1)}, f32[128,256]{1,0:T(8,128)}) custom-call(bf16[768,128]{1,0:T(8,128)(2,1)S(1)} %bitcast.12), custom_call_target="tpu_custom_call" | custom-call | tf_op jit(solution)/shard_map/pallas_call | solution.py:195
Async XLA Ops:
  0.6 14.3 %collective-permute-start = (bf16[128,256]{1,0:T(8,128)(2,1)}, bf16[128,256]{1,0:T(8,128)(2,1)S(1)}, u32[]{:S(2)}, u32[]{:S(2)}) collective-permute-start(bf16[128,256]{1,0:T(8,128)(2,1)} %bitcast.16), channel_id=1, source_target_pairs={{128,0},{129,1},{130,2},{131,3},{132,4},{133,5},{134,6},{135,7},{1... | collective-permute-start | bytes 196616 | tf_op jit(solution)/shard_map/ppermute | solution.py:190
  9.4 5.5 %copy-start.6 = (bf16[128,256]{1,0:T(8,128)(2,1)S(1)}, bf16[128,256]{1,0:T(8,128)(2,1)}, u32[]{:S(2)}) copy-start(bf16[128,256]{1,0:T(8,128)(2,1)} %loss_ref.1) | copy-start | bytes 196612
  14.9 24.9 %copy-start.4 = (f32[128,256]{1,0:T(8,128)S(1)}, f32[128,256]{1,0:T(8,128)}, u32[]{:S(2)}) copy-start(f32[128,256]{1,0:T(8,128)} %constant.29.clone.ti_ref) | copy-start | bytes 393220
  14.9 24.9 %copy-start.5 = (f32[128,256]{1,0:T(8,128)S(1)}, f32[128,256]{1,0:T(8,128)}, u32[]{:S(2)}) copy-start(f32[128,256]{1,0:T(8,128)} %constant.28.clone.tr_ref) | copy-start | bytes 393220
  14.9 24.9 %copy-start.7 = (bf16[128,256]{1,0:T(8,128)(2,1)S(1)}, bf16[128,256]{1,0:T(8,128)(2,1)}, u32[]{:S(2)}) copy-start(bf16[128,256]{1,0:T(8,128)(2,1)} %constant.35.clone.sl_ref) | copy-start | bytes 196612
  14.9 24.9 %copy-start.8 = (bf16[128,256]{1,0:T(8,128)(2,1)S(1)}, bf16[128,256]{1,0:T(8,128)(2,1)}, u32[]{:S(2)}) copy-start(bf16[128,256]{1,0:T(8,128)(2,1)} %constant.34.clone.sh_ref) | copy-start | bytes 196612
  14.9 24.9 %copy-start.9 = (bf16[256,128]{1,0:T(8,128)(2,1)S(1)}, bf16[256,128]{1,0:T(8,128)(2,1)}, u32[]{:S(2)}) copy-start(bf16[256,128]{1,0:T(8,128)(2,1)} %constant.27.clone.al_ref) | copy-start | bytes 196612
  14.9 24.9 %copy-start.10 = (bf16[256,128]{1,0:T(8,128)(2,1)S(1)}, bf16[256,128]{1,0:T(8,128)(2,1)}, u32[]{:S(2)}) copy-start(bf16[256,128]{1,0:T(8,128)(2,1)} %constant.26.clone.ah_ref) | copy-start | bytes 196612
  14.9 24.9 %copy-start.11 = (bf16[256,128]{1,0:T(8,128)(2,1)S(1)}, bf16[256,128]{1,0:T(8,128)(2,1)}, u32[]{:S(2)}) copy-start(bf16[256,128]{1,0:T(8,128)(2,1)} %constant.25.clone.gl_ref) | copy-start | bytes 196612
  15.0 24.9 %copy-start.12 = (bf16[256,128]{1,0:T(8,128)(2,1)S(1)}, bf16[256,128]{1,0:T(8,128)(2,1)}, u32[]{:S(2)}) copy-start(bf16[256,128]{1,0:T(8,128)(2,1)} %constant.24.clone.gh_ref) | copy-start | bytes 196612
  15.1 24.8 %copy-start = (bf16[256,256]{1,0:T(8,128)(2,1)S(1)}, bf16[256,256]{1,0:T(8,128)(2,1)}, u32[]{:S(2)}) copy-start(bf16[256,256]{1,0:T(8,128)(2,1)} %constant.33.clone.bl_ref) | copy-start | bytes 393220
  15.1 24.8 %copy-start.1 = (bf16[256,256]{1,0:T(8,128)(2,1)S(1)}, bf16[256,256]{1,0:T(8,128)(2,1)}, u32[]{:S(2)}) copy-start(bf16[256,256]{1,0:T(8,128)(2,1)} %constant.32.clone.bh_ref) | copy-start | bytes 393220
  15.1 24.8 %copy-start.2 = (bf16[256,256]{1,0:T(8,128)(2,1)S(1)}, bf16[256,256]{1,0:T(8,128)(2,1)}, u32[]{:S(2)}) copy-start(bf16[256,256]{1,0:T(8,128)(2,1)} %constant.31.clone.ml_ref) | copy-start | bytes 393220
  15.1 24.8 %copy-start.3 = (bf16[256,256]{1,0:T(8,128)(2,1)S(1)}, bf16[256,256]{1,0:T(8,128)(2,1)}, u32[]{:S(2)}) copy-start(bf16[256,256]{1,0:T(8,128)(2,1)} %constant.30.clone.mh_ref) | copy-start | bytes 393220

commit v4 on v3

--- a/solution.py
+++ b/solution.py
@@ -17,6 +17,7 @@
 ORDER = [int(f"{i:07b}"[::-1], 2) for i in range(BLOCK)]
 VMEM = pl.BlockSpec(memory_space=pltpu.VMEM)
 SMEM = pl.BlockSpec(memory_space=pltpu.SMEM)
+SENT_FROM = (3, 2, 0, 1)
 
 
 def halves(table):
@@ -29,7 +30,8 @@
     q = np.arange(BLOCK)
     order = np.array(ORDER)
     first = 2.0 * math.pi * np.outer(q + 0.25, order) / BLOCK
-    moved = 2.0 * math.pi * np.outer(q + 0.25, order ^ 2) / BLOCK
+    sent = order - order % 4 + np.array(SENT_FROM)[order % 4]
+    moved = 2.0 * math.pi * np.outer(q + 0.25, sent) / BLOCK
     twist = 2.0 * math.pi * np.outer(q + 0.25, q) / LENGTH
     second = 2.0 * math.pi * (np.outer(q, q) % BLOCK) / BLOCK
     gather = np.concatenate([np.cos(first), -np.sin(first)], axis=0)
@@ -68,12 +70,13 @@
         rows_ref[pl.ds(4 + half, BLOCK, stride=ROWS), :] = taps - high
 
 
-def join_kernel(rows_ref, inc_ref, loss_ref, out_ref, all_ref):
-    is_last = lax.axis_index("pipe") == lax.axis_size("pipe") - 1
+def join_kernel(rows_ref, far_ref, near_ref, loss_ref, out_ref, all_ref):
+    pipe = lax.axis_index("pipe")
     all_ref[...] = rows_ref[...]
     for half in range(2):
         lanes = slice(half * BLOCK, (half + 1) * BLOCK)
-        grad = jnp.where(is_last, loss_ref[:, lanes].astype(F32), inc_ref[:, lanes].astype(F32))
+        grad = jnp.where(pipe == 1, far_ref[:, lanes].astype(F32), near_ref[:, lanes].astype(F32))
+        grad = jnp.where(pipe == 3, loss_ref[:, lanes].astype(F32), grad)
         all_ref[pl.ds(6 + half, BLOCK, stride=ROWS), :] = grad.T
     out_ref[...] = all_ref[...].astype(BF16)
 
@@ -179,17 +182,18 @@
     return near(blocks.reshape(packed.shape))
 
 
-def route():
-    parts = lax.axis_size("pipe")
+def far_route():
     devices = lax.axis_size("seq")
-    return [(p * devices + q, (p - 1) * devices + (q ^ 2 if p == 2 else q)) for p in range(1, parts) for q in range(devices)]
+    from_of = [q - q % 4 + SENT_FROM[q % 4] for q in range(devices)]
+    return [(2 * devices + from_of[q], devices + q) for q in range(devices)]
 
 
 def per_device(layer_input, filters, skip, incoming, loss_grad):
     constants = [near(jnp.asarray(half)) for pair in tables() for half in pair]
-    passed = lax.ppermute(incoming[0], ("pipe", "seq"), route())
+    far = lax.ppermute(incoming[0], ("pipe", "seq"), far_route())
+    passed = lax.ppermute(incoming[0], "pipe", [(1, 0), (3, 2)])
     rows = call(pack_kernel, pltpu.VMEM((ROWS * BLOCK, BLOCK), F32), 3)(layer_input[0], filters[0], skip)
-    packed = call(join_kernel, packed_rows(ROWS), 3, ROW_SCRATCH)(near(rows), near(passed), near(loss_grad))
+    packed = call(join_kernel, packed_rows(ROWS), 4, ROW_SCRATCH)(near(rows), near(far), near(passed), near(loss_grad))
     results = call(main_kernel, packed_rows(BACK_ROWS), 13, ROW_SCRATCH + BACK_SCRATCH)(exchanged(packed), *constants)
     outs = (shape(BLOCK, WIDE, BF16), shape(BLOCK, WIDE, F32))
     input_grad, filter_grad = call(unpack_kernel, outs, 1, BACK_SCRATCH)(exchanged(results))

time: 59.9 us -> 60.7 us (1.013)
  starting transfers between devices: 8.75 us -> 10 us
    ppermute x1 -> x2, starting transfers between devices: 8.75 us -> 10 us  [the longest x1 8.75 us: per_device(): passed = lax.ppermute(incoming[0], 'pipe', [(1, 0), (3, 2)])]
    all_to_all x2, blocking collectives: 42 us -> 41.4 us  [exchanged(): lax.all_to_all(blocks, 'seq', split_axis=0, concat_axis=0, tiled=True, ax...]
    ppermute x1 -> x2, waiting for transfers between devices: 4.42 us -> 4.61 us  [the longest x1 4.61 us: per_device(): far = lax.ppermute(incoming[0], ('pipe', 'seq'), far_route())]
  transfers between devices with their start and end apart: 1 -> 2, of which waited for: 1 -> 1; matrix products, arithmetic and copies ran while one was open for 0% -> 0% of each run, Pallas kernels for 2% -> 2%
where the time goes in v4:
time: 60.7 us; the launch traced here: 60.5 us
  blocking collectives  41.4 us (68%)
  starting transfers between devices  10 us (16%)
  waiting for transfers between devices  4.61 us (8%)
  Pallas kernels  3.6 us (6%)
  between operations  0.83 us (1%)
    all_to_all x2, blocking collectives, exchanged(): lax.all_to_all(blocks, 'seq', split_axis=0, concat_axis=0, tiled=True, ax...  41.4 us
    ppermute x1, starting transfers between devices, per_device(): passed = lax.ppermute(incoming[0], 'pipe', [(1, 0), (3, 2)])  8.75 us
    ppermute x1, waiting for transfers between devices, per_device(): far = lax.ppermute(incoming[0], ('pipe', 'seq'), far_route())  4.61 us
    pallas_call x1, Pallas kernels, per_device(): call(main_kernel, packed_rows(BACK_ROWS), 13, ROW_SCRATCH + BACK_SCRATCH)  1.59 us
    ppermute x1, starting transfers between devices, per_device(): far = lax.ppermute(incoming[0], ('pipe', 'seq'), far_route())  1.29 us
  transfers between devices with their start and end apart: 2, of which 1 were waited for; matrix products, arithmetic and copies ran while one was open for 0% of the time, Pallas kernels for 2%

profile of v4, /device:TPU:1, one launch (start us, length us, event | category | flops | bytes accessed | tf_op | source)
XLA Modules:
  0.0 60.5 jit_solution(15722425103819765984)
XLA Ops:
  0.6 8.7 %collective-permute-start.1 = (bf16[128,256]{1,0:T(8,128)(2,1)}, bf16[128,256]{1,0:T(8,128)(2,1)S(1)}, u32[]{:S(2)}, u32[]{:S(2)}) collective-permute-start(bf16[128,256]{1,0:T(8,128)(2,1)} %bitcast.16), channel_id=1, source_target_pairs={{128,0},{384,256},{129,1},{385,257},{130,2},{386,258},{131,3},{387... | collective-permute-start | bytes 196616 | tf_op jit(solution)/shard_map/ppermute | solution.py:194
  9.4 1.3 %collective-permute-start = (bf16[128,256]{1,0:T(8,128)(2,1)}, bf16[128,256]{1,0:T(8,128)(2,1)S(1)}, u32[]{:S(2)}, u32[]{:S(2)}) collective-permute-start(bf16[128,256]{1,0:T(8,128)(2,1)} %bitcast.17), channel_id=1, source_target_pairs={{259,128},{258,129},{256,130},{257,131},{263,132},{262,133},{260,1... | collective-permute-start | bytes 196616 | tf_op jit(solution)/shard_map/ppermute | solution.py:193
  10.7 0.0 copy-start.12
  10.7 1.1 %shard_map.176.rows_ref = f32[1024,128]{1,0:T(8,128)S(1)} custom-call(bf16[128,256]{1,0:T(8,128)(2,1)} %bitcast.14, f32[128,256]{1,0:T(8,128)} %bitcast.13, f32[1,256]{1,0:T(1,128)} %skip_ref.1), custom_call_target="tpu_custom_call" | custom-call | tf_op jit(solution)/shard_map/pallas_call | solution.py:195
  11.8 0.0 collective-permute-done.1.near_ref
  11.8 4.6 %collective-permute-done.far_ref = bf16[128,256]{1,0:T(8,128)(2,1)S(1)} collective-permute-done((bf16[128,256]{1,0:T(8,128)(2,1)}, bf16[128,256]{1,0:T(8,128)(2,1)S(1)}, u32[]{:S(2)}, u32[]{:S(2)}) %collective-permute-start) | collective-permute-done | bytes 65568 | tf_op jit(solution)/shard_map/ppermute | solution.py:193
  16.4 0.0 copy-done.12
  16.4 0.0 copy-start.4
  16.4 0.0 copy-start.5
  16.4 0.0 copy-start.6
  16.4 0.0 copy-start.7
  16.4 0.0 copy-start.8
  16.4 0.0 copy-start.9
  16.4 0.0 copy-start.10
  16.5 0.0 copy-start.11
  16.5 0.1 shard_map.177
  16.6 0.0 copy-start
  16.6 0.0 copy-start.1
  16.6 0.0 copy-start.2
  16.6 0.0 copy-start.3
  16.7 24.1 %all_to_all.10 = bf16[128,8,128]{2,1,0:T(8,128)(2,1)S(1)} all-to-all(bf16[128,8,128]{2,1,0:T(8,128)(2,1)S(1)} %bitcast.10), channel_id=1, replica_groups={{0,64,32,96,16,80,48,112,8,72,40,104,24,88,56,120,4,68,36,100,20,84,52,..., dimensions={0} | all-to-all | bytes 524288 | tf_op jit(solution)/shard_map/all_to_all | solution.py:181
  40.8 0.0 copy-done.4
  40.8 0.0 copy-done.5
  40.8 0.0 copy-done.6
  40.8 0.0 copy-done.7
  40.8 0.0 copy-done.8
  40.8 0.0 copy-done.9
  40.8 0.0 copy-done.10
  40.8 0.0 copy-done.11
  40.8 0.0 copy-done
  40.9 0.0 copy-done.1
  40.9 0.0 copy-done.2
  40.9 0.0 copy-done.3
  40.9 1.6 %shard_map.178 = bf16[768,128]{1,0:T(8,128)(2,1)S(1)} custom-call(bf16[1024,128]{1,0:T(8,128)(2,1)S(1)} %bitcast.9, bf16[256,128]{1,0:T(8,128)(2,1)S(1)} %copy-done.11, bf16[256,128]{1,0:T(8,128)(2,1)S(1)} %copy-done.10, bf16[256,128]{1,0:T(8,128)(2,1)S(1)} %copy-done.9, bf16[256,128]{1,0:T(8,128)(2,1)S(1)} %copy-done.8, f32[128,256]{1,0:T(8,128)S(1)} %copy-done.5, ...), custom_call_target="tpu_custom_call" | custom-call | tf_op jit(solution)/shard_map/pallas_call | solution.py:197
  42.5 17.2 %all_to_all.11 = bf16[128,3,2,128]{3,2,1,0:T(2,128)(2,1)S(1)} all-to-all(bf16[128,3,2,128]{3,2,1,0:T(2,128)(2,1)S(1)} %bitcast.11), channel_id=1, replica_groups={{0,64,32,96,16,80,48,112,8,72,40,104,24,88,56,120,4,68,36,100,20,84,52,..., dimensions={0} | all-to-all | bytes 393216 | tf_op jit(solution)/shard_map/all_to_all | solution.py:181
  59.7 0.8 %shard_map.179 = (bf16[128,256]{1,0:T(8,128)(2,1)}, f32[128,256]{1,0:T(8,128)}) custom-call(bf16[768,128]{1,0:T(8,128)(2,1)S(1)} %bitcast.12), custom_call_target="tpu_custom_call" | custom-call | tf_op jit(solution)/shard_map/pallas_call | solution.py:199
Async XLA Ops:
  0.6 11.1 %collective-permute-start.1 = (bf16[128,256]{1,0:T(8,128)(2,1)}, bf16[128,256]{1,0:T(8,128)(2,1)S(1)}, u32[]{:S(2)}, u32[]{:S(2)}) collective-permute-start(bf16[128,256]{1,0:T(8,128)(2,1)} %bitcast.16), channel_id=1, source_target_pairs={{128,0},{384,256},{129,1},{385,257},{130,2},{386,258},{131,3},{387... | collective-permute-start | bytes 196616 | tf_op jit(solution)/shard_map/ppermute | solution.py:194
  9.4 7.0 %collective-permute-start = (bf16[128,256]{1,0:T(8,128)(2,1)}, bf16[128,256]{1,0:T(8,128)(2,1)S(1)}, u32[]{:S(2)}, u32[]{:S(2)}) collective-permute-start(bf16[128,256]{1,0:T(8,128)(2,1)} %bitcast.17), channel_id=1, source_target_pairs={{259,128},{258,129},{256,130},{257,131},{263,132},{262,133},{260,1... | collective-permute-start | bytes 196616 | tf_op jit(solution)/shard_map/ppermute | solution.py:193
  10.7 5.7 %copy-start.12 = (bf16[128,256]{1,0:T(8,128)(2,1)S(1)}, bf16[128,256]{1,0:T(8,128)(2,1)}, u32[]{:S(2)}) copy-start(bf16[128,256]{1,0:T(8,128)(2,1)} %loss_ref.1) | copy-start | bytes 196612
  16.4 24.4 %copy-start.4 = (f32[128,256]{1,0:T(8,128)S(1)}, f32[128,256]{1,0:T(8,128)}, u32[]{:S(2)}) copy-start(f32[128,256]{1,0:T(8,128)} %constant.29.clone.ti_ref) | copy-start | bytes 393220
  16.4 24.4 %copy-start.5 = (f32[128,256]{1,0:T(8,128)S(1)}, f32[128,256]{1,0:T(8,128)}, u32[]{:S(2)}) copy-start(f32[128,256]{1,0:T(8,128)} %constant.28.clone.tr_ref) | copy-start | bytes 393220
  16.4 24.4 %copy-start.6 = (bf16[128,256]{1,0:T(8,128)(2,1)S(1)}, bf16[128,256]{1,0:T(8,128)(2,1)}, u32[]{:S(2)}) copy-start(bf16[128,256]{1,0:T(8,128)(2,1)} %constant.35.clone.sl_ref) | copy-start | bytes 196612
  16.4 24.4 %copy-start.7 = (bf16[128,256]{1,0:T(8,128)(2,1)S(1)}, bf16[128,256]{1,0:T(8,128)(2,1)}, u32[]{:S(2)}) copy-start(bf16[128,256]{1,0:T(8,128)(2,1)} %constant.34.clone.sh_ref) | copy-start | bytes 196612
  16.4 24.4 %copy-start.8 = (bf16[256,128]{1,0:T(8,128)(2,1)S(1)}, bf16[256,128]{1,0:T(8,128)(2,1)}, u32[]{:S(2)}) copy-start(bf16[256,128]{1,0:T(8,128)(2,1)} %constant.27.clone.al_ref) | copy-start | bytes 196612
  16.4 24.4 %copy-start.9 = (bf16[256,128]{1,0:T(8,128)(2,1)S(1)}, bf16[256,128]{1,0:T(8,128)(2,1)}, u32[]{:S(2)}) copy-start(bf16[256,128]{1,0:T(8,128)(2,1)} %constant.26.clone.ah_ref) | copy-start | bytes 196612
  16.4 24.4 %copy-start.10 = (bf16[256,128]{1,0:T(8,128)(2,1)S(1)}, bf16[256,128]{1,0:T(8,128)(2,1)}, u32[]{:S(2)}) copy-start(bf16[256,128]{1,0:T(8,128)(2,1)} %constant.25.clone.gl_ref) | copy-start | bytes 196612
  16.5 24.4 %copy-start.11 = (bf16[256,128]{1,0:T(8,128)(2,1)S(1)}, bf16[256,128]{1,0:T(8,128)(2,1)}, u32[]{:S(2)}) copy-start(bf16[256,128]{1,0:T(8,128)(2,1)} %constant.24.clone.gh_ref) | copy-start | bytes 196612
  16.6 24.2 %copy-start = (bf16[256,256]{1,0:T(8,128)(2,1)S(1)}, bf16[256,256]{1,0:T(8,128)(2,1)}, u32[]{:S(2)}) copy-start(bf16[256,256]{1,0:T(8,128)(2,1)} %constant.33.clone.bl_ref) | copy-start | bytes 393220
  16.6 24.2 %copy-start.1 = (bf16[256,256]{1,0:T(8,128)(2,1)S(1)}, bf16[256,256]{1,0:T(8,128)(2,1)}, u32[]{:S(2)}) copy-start(bf16[256,256]{1,0:T(8,128)(2,1)} %constant.32.clone.bh_ref) | copy-start | bytes 393220
  16.6 24.2 %copy-start.2 = (bf16[256,256]{1,0:T(8,128)(2,1)S(1)}, bf16[256,256]{1,0:T(8,128)(2,1)}, u32[]{:S(2)}) copy-start(bf16[256,256]{1,0:T(8,128)(2,1)} %constant.31.clone.ml_ref) | copy-start | bytes 393220
  16.6 24.2 %copy-start.3 = (bf16[256,256]{1,0:T(8,128)(2,1)S(1)}, bf16[256,256]{1,0:T(8,128)(2,1)}, u32[]{:S(2)}) copy-start(bf16[256,256]{1,0:T(8,128)(2,1)} %constant.30.clone.mh_ref) | copy-start | bytes 393220
